TPU v7x, 128 devices: a whole 4x4x4 slice. The times are simulated.
128 devices in a mesh: sta: 8 (over x, y_hi), gx: 4 (over z), gy: 4 (over y_lo, core).
Axes of the slice: x: 4, y: 4 (y_hi: 2, y_lo: 2; y = y_hi * 2 + y_lo), z: 4, core: 2. Of those that a mesh axis runs over, the one named last changes fastest.
Arguments:
- rec_state: float32 [8, 4, 9, 32, 32, 128], P('sta', None, None, 'gx', 'gy'), may hold values from -6 to 6
- source_strain: bfloat16 [8, 8, 6, 32, 32, 128], P('sta', None, None, 'gx', 'gy'), may hold values from -6 to 6
- material: int32 [32, 32, 128], P('gx', 'gy'), may hold values from 0 to 15
- material_table: float32 [16, 3], replicated, may hold values from 0.5 to 1.5
- residual: float32 [8, 4, 8], P('sta'), may hold values from -4 to 4
- rec_cell: int32 [8, 4], P('sta'), may hold values from 0 to 1023
- listed: int32 [2, 8, 8], replicated, may hold values 0 or 1
- src_pick: int32 [2, 8], replicated, may hold values from 0 to 7
Outputs:
- kernels: float32 [2, 32, 32, 128], P(None, ('gx', 'sta'), 'gy')
All inputs are finite; a program needn't handle non-finite values.
Results may differ from a plain program's by a relative error of at most 0.0003.
Values may be sent and summed in bfloat16 or wider, within the bound.
A program may use at most 128 MiB of HBM per device.

v0:
```python
import jax
import jax.numpy as jnp
from jax import lax
from jax.sharding import PartitionSpec as P

C_NEAR = 8.0 / 12.0
C_FAR = -1.0 / 12.0
TIME_STEP = 0.25
AMPLITUDE = 4.0
KERNEL_SCALE = 0.0625
STIFFNESS = 0.3


def with_halo(block, sides, width):
    for axis, dim in sides:
        count = lax.axis_size(axis)
        forward = [(i, i + 1) for i in range(count - 1)]
        backward = [(target, source) for source, target in forward]
        low = lax.ppermute(
            lax.slice_in_dim(block, block.shape[dim] - width, None, axis=dim), axis, forward
        )
        high = lax.ppermute(lax.slice_in_dim(block, 0, width, axis=dim), axis, backward)
        block = jnp.concatenate([low, block, high], axis=dim)
    return block


def from_root(block, axis, source):
    block = jnp.where(lax.axis_index(axis) == source, block, jnp.zeros_like(block))
    return lax.psum(block, axis)


def along_first(padded):
    core = padded[..., :, 2:-2, 2:-2]
    return C_NEAR * (core[..., 3:-1, :, :] - core[..., 1:-3, :, :]) + C_FAR * (
        core[..., 4:, :, :] - core[..., :-4, :, :]
    )


def along_second(padded):
    core = padded[..., 2:-2, :, 2:-2]
    return C_NEAR * (core[..., :, 3:-1, :] - core[..., :, 1:-3, :]) + C_FAR * (
        core[..., :, 4:, :] - core[..., :, :-4, :]
    )


def along_depth(padded):
    core = padded[..., 2:-2, 2:-2, :]
    return C_NEAR * (core[..., 3:-1] - core[..., 1:-3]) + C_FAR * (core[..., 4:] - core[..., :-4])


def pad_depth(field):
    return jnp.pad(field, [(0, 0)] * (field.ndim - 1) + [(2, 2)])


def force_terms(padded, source_term):
    first = along_first(padded[:, 0]) + along_second(padded[:, 3]) + along_depth(padded[:, 4])
    second = along_first(padded[:, 3]) + along_second(padded[:, 1]) + along_depth(padded[:, 5])
    third = (
        along_first(padded[:, 4])
        + along_second(padded[:, 5])
        + along_depth(padded[:, 2])
        + source_term
    )
    return jnp.stack([first, second, third], 1)


def strain_rates(padded):
    comp_first = padded[:, 0]
    comp_second = padded[:, 1]
    comp_depth = padded[:, 2]
    rate_first = along_first(comp_first)
    rate_second = along_second(comp_second)
    rate_depth = along_depth(comp_depth)
    shear_plane = 0.5 * (along_second(comp_first) + along_first(comp_second))
    shear_first = 0.5 * (along_depth(comp_first) + along_first(comp_depth))
    shear_second = 0.5 * (along_depth(comp_second) + along_second(comp_depth))
    return jnp.stack(
        [rate_first, rate_second, rate_depth, shear_plane, shear_first, shear_second], 1
    )


def update_stress(stress, rates, lame, shear):
    trace = rates[:, 0] + rates[:, 1] + rates[:, 2]
    diagonal = stress[:, :3] + TIME_STEP * (lame * trace[:, None] + 2.0 * shear * rates[:, :3])
    offdiag = stress[:, 3:] + TIME_STEP * (2.0 * shear * rates[:, 3:])
    return jnp.concatenate([diagonal, offdiag], 1)


def correlate(source, weighted):
    trace_src = source[0] + source[1] + source[2]
    trace_rec = weighted[0] + weighted[1] + weighted[2]
    lam_part = trace_src * trace_rec
    diag_part = source[0] * weighted[0] + source[1] * weighted[1] + source[2] * weighted[2]
    off_part = source[3] * weighted[3] + source[4] * weighted[4] + source[5] * weighted[5]
    return jnp.stack([lam_part, 2.0 * diag_part + 4.0 * off_part])


def local(rec_state, source_strain, material, material_table, residual, rec_cell, listed, src_pick):
    state = rec_state[0]
    tile_x = state.shape[2]
    tile_y = state.shape[3]
    depth = state.shape[4]
    group = lax.axis_index("sta")
    count_mat = material_table.shape[0]
    onehot = (material[None] == jnp.arange(count_mat, dtype=jnp.int32)[:, None, None, None]).astype(
        jnp.float32
    )
    props = jnp.einsum("kxyz,kc->cxyz", onehot, material_table, precision=lax.Precision.HIGHEST)
    buoyancy = TIME_STEP / props[0]
    lame = STIFFNESS * props[1]
    shear = STIFFNESS * props[2]
    depth_first = (jnp.arange(depth) == 0).astype(jnp.float32)
    row_index = lax.axis_index("gx") * tile_x + jnp.arange(tile_x, dtype=jnp.int32)
    col_index = lax.axis_index("gy") * tile_y + jnp.arange(tile_y, dtype=jnp.int32)
    ny_total = lax.axis_size("gy") * tile_y
    cells = rec_cell[0]
    spots = ((cells // ny_total)[:, None, None] == row_index[None, :, None]) & (
        (cells % ny_total)[:, None, None] == col_index[None, None, :]
    )
    spots = spots.astype(jnp.float32)
    res_rows = residual[0]
    velocity = state[:, :3]
    stress = state[:, 3:]
    aggregates = []
    for moment in range(res_rows.shape[1]):
        source_term = (
            (AMPLITUDE * res_rows[:, moment])[:, None, None, None]
            * spots[:, :, :, None]
            * depth_first
        )
        stress_pad = pad_depth(with_halo(stress, (("gx", 2), ("gy", 3)), 2))
        velocity = velocity + buoyancy * force_terms(stress_pad, source_term)
        velocity_pad = pad_depth(with_halo(velocity, (("gx", 2), ("gy", 3)), 2))
        rates = strain_rates(velocity_pad)
        stress = update_stress(stress, rates, lame, shear)
        aggregates.append(
            jnp.sum((KERNEL_SCALE * res_rows[:, moment])[:, None, None, None, None] * rates, 0)
        )
    weights = lax.dynamic_slice_in_dim(listed, group, 1, 2)[:, :, 0].astype(jnp.float32)
    kernel = jnp.zeros((2, tile_x, tile_y, depth), jnp.float32)
    for rounds in range(listed.shape[0]):
        for moment in range(len(aggregates)):
            snaps = from_root(source_strain[0, moment], "sta", src_pick[rounds, moment])
            kernel = kernel + weights[rounds, moment] * correlate(
                snaps.astype(jnp.float32), aggregates[moment]
            )
    total = lax.psum(kernel, "sta")
    share = tile_x // lax.axis_size("sta")
    return lax.dynamic_slice_in_dim(total, group * share, share, 1)


def solution(mesh):
    in_specs = (
        P("sta", None, None, "gx", "gy", None),
        P("sta", None, None, "gx", "gy", None),
        P("gx", "gy", None),
        P(),
        P("sta", None, None),
        P("sta", None),
        P(),
        P(),
    )
    out_specs = P(None, ("gx", "sta"), "gy", None)
    return jax.shard_map(local, mesh=mesh, in_specs=in_specs, out_specs=out_specs, check_vma=False)
```

profile of v0, /device:TPU:0, one launch (start us, length us, event | category | flops | bytes accessed | tf_op | source)
XLA Modules:
  0.0 574.8 jit_solution(6821561108950658713)
XLA Ops:
  7.7 3.9 collective-permute-start
  23.1 3.9 collective-permute-done.3
  31.7 3.6 collective-permute-start.4
  37.5 4.3 collective-permute-done.5
  41.9 5.5 collective-permute-start.6
  48.8 2.7 collective-permute-done.7
  55.5 3.5 collective-permute-start.8
  62.2 4.4 collective-permute-done.9
  66.8 4.2 collective-permute-start.10
  72.5 2.7 collective-permute-done.11
  75.2 3.8 select_maximum_fusion.30
  85.8 4.3 collective-permute-done.13
  90.2 5.5 collective-permute-start.14
  108.8 4.4 collective-permute-done.17
  113.4 4.2 collective-permute-start.18
  121.9 3.8 select_maximum_fusion.25
  132.1 4.3 collective-permute-done.21
  136.5 5.5 collective-permute-start.22
  155.1 4.4 collective-permute-done.25
  159.7 4.2 collective-permute-start.26
  168.1 3.8 select_maximum_fusion.20
  178.4 4.3 collective-permute-done.29
  182.8 5.5 collective-permute-start.30
  201.4 4.4 collective-permute-done.33
  206.8 4.2 collective-permute-start.34
  220.3 5.5 select_maximum_fusion.15
  239.1 3.4 collective-permute-start.38
  252.6 4.5 collective-permute-start.40
  260.6 4.1 collective-permute-done.41
  265.7 5.3 collective-permute-start.42
  274.1 73.0 %all-reduce.22.cloned.1.call-done = (bf16[6,8,8,128]{3,2,1,0:T(8,128)(2,1)}, bf16[6,8,8,128]{3,2,1,0:T(8,128)(2,1)}, bf16[6,8,8,128]{3,2,1,0:T(8,128)(2,1)}, bf1...) async-done(((bf16[6,8,8,128]{3,2,1,0:T(8,128)(2,1)}, ...) | async-done | bytes 1572880 | tf_op jit(solution)/shard_map/psum | solution.py:29
  349.0 5.8 %select_maximum_fusion.10 = f32[4,6,12,12,132]{4,3,2,0,1:T(8,128)S(1)} fusion(f32[4,6,12,2,128]{4,3,2,0,1:T(2,128)} %collective-permute-done.43, f32[4,6,12,2,128]{4,3,2,0,1:T(2,128)} %collective-permute-done.42, f32[4,6,2,8,128]{4,3,2,0,1:T(8,128)} %copy-done.20, f32[4,6,2,8,128]{4,3,2,0,1:T(8,128)S(1)} %collective-permute-done.40, ...), kind=kLoop, calls=%fused_computation.14 | loop fusion | flops 6386688 | bytes 3594240 | tf_op jit(solution)/shard_map/concatenate | solution.py:23
  357.5 3.6 collective-permute-start.44
  363.3 4.3 collective-permute-done.45
  375.6 3.6 collective-permute-start.48
  382.3 4.5 collective-permute-done.49
  387.0 3.8 collective-permute-start.50
  395.0 3.8 select_maximum_fusion.5
  401.3 3.6 collective-permute-start.52
  407.1 4.3 collective-permute-done.53
  411.5 5.5 collective-permute-start.54
  429.4 4.4 collective-permute-done.57
  434.0 4.2 collective-permute-start.58
  442.5 3.8 select_maximum_fusion
  452.9 4.3 collective-permute-done.61
  457.3 5.5 collective-permute-start.62
  470.4 10.8 %fusion.647 = f32[2,8,8,128]{3,2,1,0:T(8,128)} fusion(f32[1,8,8,128]{3,2,1,0:T(8,128)S(1)} %get-tuple-element.290, f32[1,8,8,128]{3,2,1,0:T(8,128)S(1)} %get-tuple-element.289, f32[1,8,8,128]{3,2,1,0:T(8,128)S(1)} %get-tuple-element.286, f32[1,8,8,128]{3,2,1,0:T(8,128)S(1)} %get-tuple-element.285, f32[1,8,8,128]{3,2,1,0:T(8,128)S(1)} %get-tuple-element.282, ...), kind=kLoop, calls=%fused_computation.1256 | loop fusion | flops 770048 | bytes 1114176 | tf_op jit(solution)/shard_map/add | solution.py:144
  481.3 84.9 %all-reduce.20.cloned.1.call-done = f32[2,8,8,128]{3,2,1,0:T(8,128)} async-done(((f32[2,8,8,128]{3,2,1,0:T(8,128)}), f32[2,8,8,128]{3,2,1,0:T(8,128)}) %all-reduce.20.cloned.1.call-update) | async-done | bytes 65552 | tf_op jit(solution)/shard_map/psum | solution.py:147
  (410 shorter events, 186.0 us)
Async XLA Ops:
  6.5 340.5 %all-reduce.22.cloned.1.call-start = ((), (), s32[]{:S(2)}) async-start(), calls=%async_computation.1 | async-start | bytes 3145728 | tf_op jit(solution)/shard_map/psum | solution.py:29
  7.7 9.9 %collective-permute-start = (f32[4,6,2,8,128]{4,3,2,0,1:T(8,128)S(1)}, f32[4,6,2,8,128]{4,3,2,0,1:T(8,128)S(1)}, u32[]{:S(2)}, u32[]{:S(2)}) collective-permute-start(f32[4,6,2,8,128]{4,3,2,0,1:T(8,128)S(1)} %copy.59), channel_id=1, source_target_pairs={{0,4},{4,8},{8,12},{1,5},{5,9},{9,13},{2,6},{6,10},{10,14},{3,7},{... | collective-permute-start | bytes 589832 | tf_op jit(solution)/shard_map/ppermute | solution.py:19
  11.7 8.4 %collective-permute-start.1 = (f32[4,6,2,8,128]{4,3,2,0,1:T(8,128)S(1)}, f32[4,6,2,8,128]{4,3,2,0,1:T(8,128)S(1)}, u32[]{:S(2)}, u32[]{:S(2)}) collective-permute-start(f32[4,6,2,8,128]{4,3,2,0,1:T(8,128)S(1)} %copy.61), channel_id=1, source_target_pairs={{4,0},{8,4},{12,8},{5,1},{9,5},{13,9},{6,2},{10,6},{14,10},{7,3},{... | collective-permute-start | bytes 589832 | tf_op jit(solution)/shard_map/ppermute | solution.py:22
  21.7 5.3 collective-permute-start.3
  31.7 5.8 %collective-permute-start.4 = (f32[4,3,2,8,128]{4,3,2,0,1:T(8,128)S(1)}, f32[4,3,2,8,128]{4,3,2,0,1:T(8,128)S(1)}, u32[]{:S(2)}, u32[]{:S(2)}) collective-permute-start(f32[4,3,2,8,128]{4,3,2,0,1:T(8,128)S(1)} %get-tuple-element.291), channel_id=1, source_target_pairs={{0,4},{4,8},{8,12},{1,5},{5,9},{9,13},{2,6},{6,10},{10,14},{3,7},{... | collective-permute-start | bytes 294920 | tf_op jit(solution)/shard_map/ppermute | solution.py:19
  35.3 6.5 %collective-permute-start.5 = (f32[4,3,2,8,128]{4,3,2,0,1:T(8,128)S(1)}, f32[4,3,2,8,128]{4,3,2,0,1:T(8,128)S(1)}, u32[]{:S(2)}, u32[]{:S(2)}) collective-permute-start(f32[4,3,2,8,128]{4,3,2,0,1:T(8,128)S(1)} %get-tuple-element.292), channel_id=1, source_target_pairs={{4,0},{8,4},{12,8},{5,1},{9,5},{13,9},{6,2},{10,6},{14,10},{7,3},{... | collective-permute-start | bytes 294920 | tf_op jit(solution)/shard_map/ppermute | solution.py:22
  41.9 6.9 %collective-permute-start.6 = (f32[4,3,12,2,128]{4,3,2,0,1:T(2,128)S(1)}, f32[4,3,12,2,128]{4,3,2,0,1:T(2,128)S(1)}, u32[]{:S(2)}, u32[]{:S(2)}) collective-permute-start(f32[4,3,12,2,128]{4,3,2,0,1:T(2,128)S(1)} %get-tuple-element.243), channel_id=1, source_target_pairs={{0,1},{1,2},{2,3},{4,5},{5,6},{6,7},{8,9},{9,10},{10,11},{12,13},{... | collective-permute-start | bytes 442376 | tf_op jit(solution)/shard_map/ppermute | solution.py:19
  55.5 6.7 %collective-permute-start.8 = (f32[4,6,2,8,128]{4,3,2,0,1:T(8,128)S(1)}, f32[4,6,2,8,128]{4,3,2,0,1:T(8,128)S(1)}, u32[]{:S(2)}, u32[]{:S(2)}) collective-permute-start(f32[4,6,2,8,128]{4,3,2,0,1:T(8,128)S(1)} %get-tuple-element.211), channel_id=1, source_target_pairs={{0,4},{4,8},{8,12},{1,5},{5,9},{9,13},{2,6},{6,10},{10,14},{3,7},{... | collective-permute-start | bytes 589832 | tf_op jit(solution)/shard_map/ppermute | solution.py:19
  59.0 7.6 %collective-permute-start.9 = (f32[4,6,2,8,128]{4,3,2,0,1:T(8,128)S(1)}, f32[4,6,2,8,128]{4,3,2,0,1:T(8,128)S(1)}, u32[]{:S(2)}, u32[]{:S(2)}) collective-permute-start(f32[4,6,2,8,128]{4,3,2,0,1:T(8,128)S(1)} %get-tuple-element.212), channel_id=1, source_target_pairs={{4,0},{8,4},{12,8},{5,1},{9,5},{13,9},{6,2},{10,6},{14,10},{7,3},{... | collective-permute-start | bytes 589832 | tf_op jit(solution)/shard_map/ppermute | solution.py:22
  66.8 5.7 collective-permute-start.10
  81.2 4.6 collective-permute-start.12
  83.6 6.5 %collective-permute-start.13 = (f32[4,3,2,8,128]{4,3,2,0,1:T(8,128)S(1)}, f32[4,3,2,8,128]{4,3,2,0,1:T(8,128)S(1)}, u32[]{:S(2)}, u32[]{:S(2)}) collective-permute-start(f32[4,3,2,8,128]{4,3,2,0,1:T(8,128)S(1)} %get-tuple-element.288), channel_id=1, source_target_pairs={{4,0},{8,4},{12,8},{5,1},{9,5},{13,9},{6,2},{10,6},{14,10},{7,3},{... | collective-permute-start | bytes 294920 | tf_op jit(solution)/shard_map/ppermute | solution.py:22
  90.2 6.9 %collective-permute-start.14 = (f32[4,3,12,2,128]{4,3,2,0,1:T(2,128)S(1)}, f32[4,3,12,2,128]{4,3,2,0,1:T(2,128)S(1)}, u32[]{:S(2)}, u32[]{:S(2)}) collective-permute-start(f32[4,3,12,2,128]{4,3,2,0,1:T(2,128)S(1)} %get-tuple-element.241), channel_id=1, source_target_pairs={{0,1},{1,2},{2,3},{4,5},{5,6},{6,7},{8,9},{9,10},{10,11},{12,13},{... | collective-permute-start | bytes 442376 | tf_op jit(solution)/shard_map/ppermute | solution.py:19
  103.7 5.1 collective-permute-start.16
  105.7 7.6 %collective-permute-start.17 = (f32[4,6,2,8,128]{4,3,2,0,1:T(8,128)S(1)}, f32[4,6,2,8,128]{4,3,2,0,1:T(8,128)S(1)}, u32[]{:S(2)}, u32[]{:S(2)}) collective-permute-start(f32[4,6,2,8,128]{4,3,2,0,1:T(8,128)S(1)} %get-tuple-element.210), channel_id=1, source_target_pairs={{4,0},{8,4},{12,8},{5,1},{9,5},{13,9},{6,2},{10,6},{14,10},{7,3},{... | collective-permute-start | bytes 589832 | tf_op jit(solution)/shard_map/ppermute | solution.py:22
  113.4 5.8 %collective-permute-start.18 = (f32[4,6,12,2,128]{4,3,2,0,1:T(2,128)S(1)}, f32[4,6,12,2,128]{4,3,2,0,1:T(2,128)S(1)}, u32[]{:S(2)}, u32[]{:S(2)}) collective-permute-start(f32[4,6,12,2,128]{4,3,2,0,1:T(2,128)S(1)} %get-tuple-element.189), channel_id=1, source_target_pairs={{0,1},{1,2},{2,3},{4,5},{5,6},{6,7},{8,9},{9,10},{10,11},{12,13},{... | collective-permute-start | bytes 884744 | tf_op jit(solution)/shard_map/ppermute | solution.py:19
  129.9 6.5 %collective-permute-start.21 = (f32[4,3,2,8,128]{4,3,2,0,1:T(8,128)S(1)}, f32[4,3,2,8,128]{4,3,2,0,1:T(8,128)S(1)}, u32[]{:S(2)}, u32[]{:S(2)}) collective-permute-start(f32[4,3,2,8,128]{4,3,2,0,1:T(8,128)S(1)} %get-tuple-element.284), channel_id=1, source_target_pairs={{4,0},{8,4},{12,8},{5,1},{9,5},{13,9},{6,2},{10,6},{14,10},{7,3},{... | collective-permute-start | bytes 294920 | tf_op jit(solution)/shard_map/ppermute | solution.py:22
  136.5 6.9 %collective-permute-start.22 = (f32[4,3,12,2,128]{4,3,2,0,1:T(2,128)S(1)}, f32[4,3,12,2,128]{4,3,2,0,1:T(2,128)S(1)}, u32[]{:S(2)}, u32[]{:S(2)}) collective-permute-start(f32[4,3,12,2,128]{4,3,2,0,1:T(2,128)S(1)} %get-tuple-element.239), channel_id=1, source_target_pairs={{0,1},{1,2},{2,3},{4,5},{5,6},{6,7},{8,9},{9,10},{10,11},{12,13},{... | collective-permute-start | bytes 442376 | tf_op jit(solution)/shard_map/ppermute | solution.py:19
  150.0 5.1 collective-permute-start.24
  151.9 7.6 %collective-permute-start.25 = (f32[4,6,2,8,128]{4,3,2,0,1:T(8,128)S(1)}, f32[4,6,2,8,128]{4,3,2,0,1:T(8,128)S(1)}, u32[]{:S(2)}, u32[]{:S(2)}) collective-permute-start(f32[4,6,2,8,128]{4,3,2,0,1:T(8,128)S(1)} %get-tuple-element.208), channel_id=1, source_target_pairs={{4,0},{8,4},{12,8},{5,1},{9,5},{13,9},{6,2},{10,6},{14,10},{7,3},{... | collective-permute-start | bytes 589832 | tf_op jit(solution)/shard_map/ppermute | solution.py:22
  159.7 6.0 %collective-permute-start.26 = (f32[4,6,12,2,128]{4,3,2,0,1:T(2,128)S(1)}, f32[4,6,12,2,128]{4,3,2,0,1:T(2,128)S(1)}, u32[]{:S(2)}, u32[]{:S(2)}) collective-permute-start(f32[4,6,12,2,128]{4,3,2,0,1:T(2,128)S(1)} %get-tuple-element.187), channel_id=1, source_target_pairs={{0,1},{1,2},{2,3},{4,5},{5,6},{6,7},{8,9},{9,10},{10,11},{12,13},{... | collective-permute-start | bytes 884744 | tf_op jit(solution)/shard_map/ppermute | solution.py:19
  176.2 6.5 %collective-permute-start.29 = (f32[4,3,2,8,128]{4,3,2,0,1:T(8,128)S(1)}, f32[4,3,2,8,128]{4,3,2,0,1:T(8,128)S(1)}, u32[]{:S(2)}, u32[]{:S(2)}) collective-permute-start(f32[4,3,2,8,128]{4,3,2,0,1:T(8,128)S(1)} %get-tuple-element.280), channel_id=1, source_target_pairs={{4,0},{8,4},{12,8},{5,1},{9,5},{13,9},{6,2},{10,6},{14,10},{7,3},{... | collective-permute-start | bytes 294920 | tf_op jit(solution)/shard_map/ppermute | solution.py:22
  182.8 6.9 %collective-permute-start.30 = (f32[4,3,12,2,128]{4,3,2,0,1:T(2,128)S(1)}, f32[4,3,12,2,128]{4,3,2,0,1:T(2,128)S(1)}, u32[]{:S(2)}, u32[]{:S(2)}) collective-permute-start(f32[4,3,12,2,128]{4,3,2,0,1:T(2,128)S(1)} %get-tuple-element.237), channel_id=1, source_target_pairs={{0,1},{1,2},{2,3},{4,5},{5,6},{6,7},{8,9},{9,10},{10,11},{12,13},{... | collective-permute-start | bytes 442376 | tf_op jit(solution)/shard_map/ppermute | solution.py:19
  196.3 5.1 collective-permute-start.32
  198.2 7.6 %collective-permute-start.33 = (f32[4,6,2,8,128]{4,3,2,0,1:T(8,128)S(1)}, f32[4,6,2,8,128]{4,3,2,0,1:T(8,128)S(1)}, u32[]{:S(2)}, u32[]{:S(2)}) collective-permute-start(f32[4,6,2,8,128]{4,3,2,0,1:T(8,128)S(1)} %get-tuple-element.206), channel_id=1, source_target_pairs={{4,0},{8,4},{12,8},{5,1},{9,5},{13,9},{6,2},{10,6},{14,10},{7,3},{... | collective-permute-start | bytes 589832 | tf_op jit(solution)/shard_map/ppermute | solution.py:22
  206.8 13.4 %collective-permute-start.34 = (f32[4,6,12,2,128]{4,3,2,0,1:T(2,128)}, f32[4,6,12,2,128]{4,3,2,0,1:T(2,128)S(1)}, u32[]{:S(2)}, u32[]{:S(2)}) collective-permute-start(f32[4,6,12,2,128]{4,3,2,0,1:T(2,128)} %get-tuple-element.185), channel_id=1, source_target_pairs={{0,1},{1,2},{2,3},{4,5},{5,6},{6,7},{8,9},{9,10},{10,11},{12,13},{... | collective-permute-start | bytes 884744 | tf_op jit(solution)/shard_map/ppermute | solution.py:19
  211.0 9.3 %collective-permute-start.35 = (f32[4,6,12,2,128]{4,3,2,0,1:T(2,128)}, f32[4,6,12,2,128]{4,3,2,0,1:T(2,128)}, u32[]{:S(2)}, u32[]{:S(2)}) collective-permute-start(f32[4,6,12,2,128]{4,3,2,0,1:T(2,128)} %get-tuple-element.186), channel_id=1, source_target_pairs={{1,0},{2,1},{3,2},{5,4},{6,5},{7,6},{9,8},{10,9},{11,10},{13,12},{... | collective-permute-start | bytes 884744 | tf_op jit(solution)/shard_map/ppermute | solution.py:22
  228.9 8.8 %collective-permute-start.36 = (f32[4,3,2,8,128]{4,3,2,0,1:T(8,128)}, f32[4,3,2,8,128]{4,3,2,0,1:T(8,128)S(1)}, u32[]{:S(2)}, u32[]{:S(2)}) collective-permute-start(f32[4,3,2,8,128]{4,3,2,0,1:T(8,128)} %get-tuple-element.275), channel_id=1, source_target_pairs={{0,4},{4,8},{8,12},{1,5},{5,9},{9,13},{2,6},{6,10},{10,14},{3,7},{... | collective-permute-start | bytes 294920 | tf_op jit(solution)/shard_map/ppermute | solution.py:19
  231.1 7.2 %collective-permute-start.37 = (f32[4,3,2,8,128]{4,3,2,0,1:T(8,128)S(1)}, f32[4,3,2,8,128]{4,3,2,0,1:T(8,128)S(1)}, u32[]{:S(2)}, u32[]{:S(2)}) collective-permute-start(f32[4,3,2,8,128]{4,3,2,0,1:T(8,128)S(1)} %get-tuple-element.276), channel_id=1, source_target_pairs={{4,0},{8,4},{12,8},{5,1},{9,5},{13,9},{6,2},{10,6},{14,10},{7,3},{... | collective-permute-start | bytes 294920 | tf_op jit(solution)/shard_map/ppermute | solution.py:22
  239.1 6.8 %collective-permute-start.38 = (f32[4,3,12,2,128]{4,3,2,0,1:T(2,128)}, f32[4,3,12,2,128]{4,3,2,0,1:T(2,128)}, u32[]{:S(2)}, u32[]{:S(2)}) collective-permute-start(f32[4,3,12,2,128]{4,3,2,0,1:T(2,128)} %get-tuple-element.235), channel_id=1, source_target_pairs={{0,1},{1,2},{2,3},{4,5},{5,6},{6,7},{8,9},{9,10},{10,11},{12,13},{... | collective-permute-start | bytes 442376 | tf_op jit(solution)/shard_map/ppermute | solution.py:19
  245.9 320.3 %all-reduce.20.cloned.1.call-start = ((), (), s32[]{:S(2)}) async-start(), calls=%async_computation | async-start | bytes 131072 | tf_op jit(solution)/shard_map/psum | solution.py:147
  252.6 8.0 %collective-permute-start.40 = (f32[4,6,2,8,128]{4,3,2,0,1:T(8,128)}, f32[4,6,2,8,128]{4,3,2,0,1:T(8,128)S(1)}, u32[]{:S(2)}, u32[]{:S(2)}) collective-permute-start(f32[4,6,2,8,128]{4,3,2,0,1:T(8,128)} %get-tuple-element.203), channel_id=1, source_target_pairs={{0,4},{4,8},{8,12},{1,5},{5,9},{9,13},{2,6},{6,10},{10,14},{3,7},{... | collective-permute-start | bytes 589832 | tf_op jit(solution)/shard_map/ppermute | solution.py:19
  257.1 7.6 %collective-permute-start.41 = (f32[4,6,2,8,128]{4,3,2,0,1:T(8,128)S(1)}, f32[4,6,2,8,128]{4,3,2,0,1:T(8,128)S(1)}, u32[]{:S(2)}, u32[]{:S(2)}) collective-permute-start(f32[4,6,2,8,128]{4,3,2,0,1:T(8,128)S(1)} %get-tuple-element.204), channel_id=1, source_target_pairs={{4,0},{8,4},{12,8},{5,1},{9,5},{13,9},{6,2},{10,6},{14,10},{7,3},{... | collective-permute-start | bytes 589832 | tf_op jit(solution)/shard_map/ppermute | solution.py:22
  265.7 83.3 %collective-permute-start.42 = (f32[4,6,12,2,128]{4,3,2,0,1:T(2,128)}, f32[4,6,12,2,128]{4,3,2,0,1:T(2,128)}, u32[]{:S(2)}, u32[]{:S(2)}) collective-permute-start(f32[4,6,12,2,128]{4,3,2,0,1:T(2,128)} %get-tuple-element.183), channel_id=1, source_target_pairs={{0,1},{1,2},{2,3},{4,5},{5,6},{6,7},{8,9},{9,10},{10,11},{12,13},{... | collective-permute-start | bytes 884744 | tf_op jit(solution)/shard_map/ppermute | solution.py:19
  270.9 78.0 %collective-permute-start.43 = (f32[4,6,12,2,128]{4,3,2,0,1:T(2,128)}, f32[4,6,12,2,128]{4,3,2,0,1:T(2,128)}, u32[]{:S(2)}, u32[]{:S(2)}) collective-permute-start(f32[4,6,12,2,128]{4,3,2,0,1:T(2,128)} %get-tuple-element.184), channel_id=1, source_target_pairs={{1,0},{2,1},{3,2},{5,4},{6,5},{7,6},{9,8},{10,9},{11,10},{13,12},{... | collective-permute-start | bytes 884744 | tf_op jit(solution)/shard_map/ppermute | solution.py:22
  357.5 5.8 %collective-permute-start.44 = (f32[4,3,2,8,128]{4,3,2,0,1:T(8,128)S(1)}, f32[4,3,2,8,128]{4,3,2,0,1:T(8,128)S(1)}, u32[]{:S(2)}, u32[]{:S(2)}) collective-permute-start(f32[4,3,2,8,128]{4,3,2,0,1:T(8,128)S(1)} %get-tuple-element.271), channel_id=1, source_target_pairs={{0,4},{4,8},{8,12},{1,5},{5,9},{9,13},{2,6},{6,10},{10,14},{3,7},{... | collective-permute-start | bytes 294920 | tf_op jit(solution)/shard_map/ppermute | solution.py:19
  361.1 6.5 %collective-permute-start.45 = (f32[4,3,2,8,128]{4,3,2,0,1:T(8,128)S(1)}, f32[4,3,2,8,128]{4,3,2,0,1:T(8,128)S(1)}, u32[]{:S(2)}, u32[]{:S(2)}) collective-permute-start(f32[4,3,2,8,128]{4,3,2,0,1:T(8,128)S(1)} %get-tuple-element.272), channel_id=1, source_target_pairs={{4,0},{8,4},{12,8},{5,1},{9,5},{13,9},{6,2},{10,6},{14,10},{7,3},{... | collective-permute-start | bytes 294920 | tf_op jit(solution)/shard_map/ppermute | solution.py:22
  375.6 6.8 %collective-permute-start.48 = (f32[4,6,2,8,128]{4,3,2,0,1:T(8,128)S(1)}, f32[4,6,2,8,128]{4,3,2,0,1:T(8,128)S(1)}, u32[]{:S(2)}, u32[]{:S(2)}) collective-permute-start(f32[4,6,2,8,128]{4,3,2,0,1:T(8,128)S(1)} %get-tuple-element.201), channel_id=1, source_target_pairs={{0,4},{4,8},{8,12},{1,5},{5,9},{9,13},{2,6},{6,10},{10,14},{3,7},{... | collective-permute-start | bytes 589832 | tf_op jit(solution)/shard_map/ppermute | solution.py:19
  379.2 7.6 %collective-permute-start.49 = (f32[4,6,2,8,128]{4,3,2,0,1:T(8,128)S(1)}, f32[4,6,2,8,128]{4,3,2,0,1:T(8,128)S(1)}, u32[]{:S(2)}, u32[]{:S(2)}) collective-permute-start(f32[4,6,2,8,128]{4,3,2,0,1:T(8,128)S(1)} %get-tuple-element.202), channel_id=1, source_target_pairs={{4,0},{8,4},{12,8},{5,1},{9,5},{13,9},{6,2},{10,6},{14,10},{7,3},{... | collective-permute-start | bytes 589832 | tf_op jit(solution)/shard_map/ppermute | solution.py:22
  387.0 5.7 collective-permute-start.50
  401.3 5.8 %collective-permute-start.52 = (f32[4,3,2,8,128]{4,3,2,0,1:T(8,128)S(1)}, f32[4,3,2,8,128]{4,3,2,0,1:T(8,128)S(1)}, u32[]{:S(2)}, u32[]{:S(2)}) collective-permute-start(f32[4,3,2,8,128]{4,3,2,0,1:T(8,128)S(1)} %get-tuple-element.267), channel_id=1, source_target_pairs={{0,4},{4,8},{8,12},{1,5},{5,9},{9,13},{2,6},{6,10},{10,14},{3,7},{... | collective-permute-start | bytes 294920 | tf_op jit(solution)/shard_map/ppermute | solution.py:19
  404.9 6.5 %collective-permute-start.53 = (f32[4,3,2,8,128]{4,3,2,0,1:T(8,128)S(1)}, f32[4,3,2,8,128]{4,3,2,0,1:T(8,128)S(1)}, u32[]{:S(2)}, u32[]{:S(2)}) collective-permute-start(f32[4,3,2,8,128]{4,3,2,0,1:T(8,128)S(1)} %get-tuple-element.268), channel_id=1, source_target_pairs={{4,0},{8,4},{12,8},{5,1},{9,5},{13,9},{6,2},{10,6},{14,10},{7,3},{... | collective-permute-start | bytes 294920 | tf_op jit(solution)/shard_map/ppermute | solution.py:22
  411.5 6.9 %collective-permute-start.54 = (f32[4,3,12,2,128]{4,3,2,0,1:T(2,128)S(1)}, f32[4,3,12,2,128]{4,3,2,0,1:T(2,128)S(1)}, u32[]{:S(2)}, u32[]{:S(2)}) collective-permute-start(f32[4,3,12,2,128]{4,3,2,0,1:T(2,128)S(1)} %get-tuple-element.231), channel_id=1, source_target_pairs={{0,1},{1,2},{2,3},{4,5},{5,6},{6,7},{8,9},{9,10},{10,11},{12,13},{... | collective-permute-start | bytes 442376 | tf_op jit(solution)/shard_map/ppermute | solution.py:19
  424.3 5.1 collective-permute-start.56
  426.3 7.6 %collective-permute-start.57 = (f32[4,6,2,8,128]{4,3,2,1,0:T(8,128)S(1)}, f32[4,6,2,8,128]{4,3,2,1,0:T(8,128)S(1)}, u32[]{:S(2)}, u32[]{:S(2)}) collective-permute-start(f32[4,6,2,8,128]{4,3,2,1,0:T(8,128)S(1)} %get-tuple-element.200), channel_id=1, source_target_pairs={{4,0},{8,4},{12,8},{5,1},{9,5},{13,9},{6,2},{10,6},{14,10},{7,3},{... | collective-permute-start | bytes 589832 | tf_op jit(solution)/shard_map/ppermute | solution.py:22
  434.0 5.9 %collective-permute-start.58 = (f32[4,6,12,2,128]{4,3,2,1,0:T(2,128)S(1)}, f32[4,6,12,2,128]{4,3,2,1,0:T(2,128)S(1)}, u32[]{:S(2)}, u32[]{:S(2)}) collective-permute-start(f32[4,6,12,2,128]{4,3,2,1,0:T(2,128)S(1)} %get-tuple-element.179), channel_id=1, source_target_pairs={{0,1},{1,2},{2,3},{4,5},{5,6},{6,7},{8,9},{9,10},{10,11},{12,13},{... | collective-permute-start | bytes 884744 | tf_op jit(solution)/shard_map/ppermute | solution.py:19
  450.7 6.5 %collective-permute-start.61 = (f32[4,3,2,8,128]{4,3,2,0,1:T(8,128)S(1)}, f32[4,3,2,8,128]{4,3,2,0,1:T(8,128)S(1)}, u32[]{:S(2)}, u32[]{:S(2)}) collective-permute-start(f32[4,3,2,8,128]{4,3,2,0,1:T(8,128)S(1)} %get-tuple-element.264), channel_id=1, source_target_pairs={{4,0},{8,4},{12,8},{5,1},{9,5},{13,9},{6,2},{10,6},{14,10},{7,3},{... | collective-permute-start | bytes 294920 | tf_op jit(solution)/shard_map/ppermute | solution.py:22
  457.3 6.9 %collective-permute-start.62 = (f32[4,3,12,2,128]{4,3,2,0,1:T(2,128)S(1)}, f32[4,3,12,2,128]{4,3,2,0,1:T(2,128)S(1)}, u32[]{:S(2)}, u32[]{:S(2)}) collective-permute-start(f32[4,3,12,2,128]{4,3,2,0,1:T(2,128)S(1)} %get-tuple-element.229), channel_id=1, source_target_pairs={{0,1},{1,2},{2,3},{4,5},{5,6},{6,7},{8,9},{9,10},{10,11},{12,13},{... | collective-permute-start | bytes 442376 | tf_op jit(solution)/shard_map/ppermute | solution.py:19
  (68 other events, 666.9 us)
Sparse Core Ops, SparseCore 0:
  246.0 101.0 all-reduce.21
  481.4 84.7 all-reduce.19
where the time goes:
time: 585 us; the launch traced here: 575 us
  waiting for transfers between devices  275 us (47%)
  starting transfers between devices  157 us (27%)
  other arithmetic  96.7 us (17%)
  between operations  26.7 us (5%)
  local copies, waits for them, and re-layouts  18.2 us (3%)
    ppermute x32, starting transfers between devices, with_halo(): lax.ppermute(lax.slice_in_dim(block, block.shape[dim] - width, None, axis...  114 us
    ppermute x32, waiting for transfers between devices, with_halo(): lax.ppermute(lax.slice_in_dim(block, 0, width, axis=dim), axis, backward)  99.5 us
    psum x1, waiting for transfers between devices, local(): total = lax.psum(kernel, 'sta')  84.9 us
    psum x1, waiting for transfers between devices, from_root(): return lax.psum(block, axis)  73 us
    concatenate x16, other arithmetic, with_halo(): block = jnp.concatenate([low, block, high], axis=dim)  43.9 us
    ppermute x32, starting transfers between devices, with_halo(): lax.ppermute(lax.slice_in_dim(block, 0, width, axis=dim), axis, backward)  43.2 us
    ppermute x32, waiting for transfers between devices, with_halo(): lax.ppermute(lax.slice_in_dim(block, block.shape[dim] - width, None, axis...  17.8 us
  transfers between devices with their start and end apart: 66, of which 46 were waited for; matrix products, arithmetic and copies ran while one was open for 4% of the time, Pallas kernels for 0%

commit v1 on v0

--- a/solution.py
+++ b/solution.py
@@ -144,7 +144,7 @@
             kernel = kernel + weights[rounds, moment] * correlate(
                 snaps.astype(jnp.float32), aggregates[moment]
             )
-    total = lax.psum(kernel, "sta")
+    total = jnp.sum(lax.all_gather(kernel, "sta"), axis=0)
     share = tile_x // lax.axis_size("sta")
     return lax.dynamic_slice_in_dim(total, group * share, share, 1)
 

time: 585 us -> 536 us (0.916)
  the two profiles are of different devices: /device:TPU:0 before, /device:TPU:8 now
where the time goes in v1:
time: 536 us; the launch traced here: 526 us
  waiting for transfers between devices  194 us (36%)
  starting transfers between devices  155 us (29%)
  other arithmetic  96 us (18%)
  blocking collectives  35.2 us (7%)
  between operations  26.6 us (5%)
  local copies, waits for them, and re-layouts  17.5 us (3%)
    ppermute x32, waiting for transfers between devices, with_halo(): lax.ppermute(lax.slice_in_dim(block, 0, width, axis=dim), axis, backward)  86.9 us
    ppermute x32, starting transfers between devices, with_halo(): lax.ppermute(lax.slice_in_dim(block, 0, width, axis=dim), axis, backward)  80.8 us
    ppermute x32, starting transfers between devices, with_halo(): lax.ppermute(lax.slice_in_dim(block, block.shape[dim] - width, None, axis...  74.4 us
    psum x1, waiting for transfers between devices, from_root(): return lax.psum(block, axis)  70.7 us
    concatenate x16, other arithmetic, with_halo(): block = jnp.concatenate([low, block, high], axis=dim)  43.9 us
    ppermute x32, waiting for transfers between devices, with_halo(): lax.ppermute(lax.slice_in_dim(block, block.shape[dim] - width, None, axis...  36.7 us
    all_gather x1, blocking collectives, local(): total = jnp.sum(lax.all_gather(kernel, 'sta'), axis=0)  35.2 us
    another operation x24, other arithmetic, force_terms(): return jnp.stack([first, second, third], 1)  10.9 us
  transfers between devices with their start and end apart: 65, of which 57 were waited for; matrix products, arithmetic and copies ran while one was open for 4% of the time, Pallas kernels for 0%

profile of v1, /device:TPU:8, one launch (start us, length us, event | category | flops | bytes accessed | tf_op | source)
XLA Modules:
  0.0 525.7 jit_solution(9666781851564022117)
XLA Ops:
  7.7 3.8 collective-permute-start
  22.2 3.6 collective-permute-start.3
  30.0 2.5 select_maximum_fusion.35
  34.8 3.6 collective-permute-start.4
  40.6 4.3 collective-permute-done.5
  47.0 3.6 collective-permute-start.7
  57.2 3.5 collective-permute-start.8
  63.9 4.4 collective-permute-done.9
  70.4 3.9 collective-permute-start.11
  78.3 3.8 select_maximum_fusion.30
  88.9 4.3 collective-permute-done.13
  95.3 3.6 collective-permute-start.15
  110.6 4.4 collective-permute-done.17
  117.1 3.9 collective-permute-start.19
  125.0 3.8 select_maximum_fusion.25
  135.2 4.3 collective-permute-done.21
  141.5 3.6 collective-permute-start.23
  156.8 4.4 collective-permute-done.25
  163.4 4.1 collective-permute-start.27
  171.2 3.8 select_maximum_fusion.20
  181.5 4.3 collective-permute-done.29
  187.8 3.6 collective-permute-start.31
  203.2 4.4 collective-permute-done.33
  210.5 3.8 collective-permute-start.35
  222.1 5.5 %select_maximum_fusion.15 = f32[4,6,12,12,132]{4,3,2,0,1:T(8,128)S(1)} fusion(f32[4,6,12,2,128]{4,3,2,0,1:T(2,128)} %collective-permute-done.35, f32[4,6,12,2,128]{4,3,2,0,1:T(2,128)S(1)} %collective-permute-done.34, f32[4,6,2,8,128]{4,3,2,0,1:T(8,128)S(1)} %collective-permute-done.33, f32[4,6,2,8,128]{4,3,2,0,1:T(8,128)S(1)} %collective-permute-done.32, ...), kind=kLoop, calls=%fused_computation.19 | loop fusion | flops 6386688 | bytes 3594240 | tf_op jit(solution)/shard_map/concatenate | solution.py:23
  242.1 3.6 collective-permute-start.39
  254.3 4.5 collective-permute-start.40
  262.3 4.1 collective-permute-done.41
  269.4 3.9 collective-permute-start.43
  274.9 70.7 %all-reduce.19.cloned.1.call-done = (bf16[6,8,8,128]{3,2,1,0:T(8,128)(2,1)}, bf16[6,8,8,128]{3,2,1,0:T(8,128)(2,1)}, bf16[6,8,8,128]{3,2,1,0:T(8,128)(2,1)}, bf1...) async-done(((bf16[6,8,8,128]{3,2,1,0:T(8,128)(2,1)}, ...) | async-done | bytes 1572880 | tf_op jit(solution)/shard_map/psum | solution.py:29
  347.5 5.8 %select_maximum_fusion.10 = f32[4,6,12,12,132]{4,3,2,0,1:T(8,128)S(1)} fusion(f32[4,6,12,2,128]{4,3,2,0,1:T(2,128)} %collective-permute-done.43, f32[4,6,12,2,128]{4,3,2,0,1:T(2,128)} %collective-permute-done.42, f32[4,6,2,8,128]{4,3,2,0,1:T(8,128)} %copy-done.20, f32[4,6,2,8,128]{4,3,2,0,1:T(8,128)S(1)} %collective-permute-done.40, ...), kind=kLoop, calls=%fused_computation.14 | loop fusion | flops 6386688 | bytes 3594240 | tf_op jit(solution)/shard_map/concatenate | solution.py:23
  356.1 3.1 collective-permute-start.44
  361.4 4.3 collective-permute-done.45
  367.7 3.6 collective-permute-start.47
  377.3 3.6 collective-permute-start.48
  384.0 4.4 collective-permute-done.49
  390.6 3.9 collective-permute-start.51
  398.4 3.8 select_maximum_fusion.5
  404.7 3.6 collective-permute-start.52
  410.6 4.3 collective-permute-done.53
  416.9 3.6 collective-permute-start.55
  431.5 4.4 collective-permute-done.57
  438.1 3.9 collective-permute-start.59
  445.9 3.8 select_maximum_fusion
  456.4 4.3 collective-permute-done.61
  462.7 3.6 collective-permute-start.63
  472.5 10.0 %fusion.647 = f32[1,2,8,8,128]{4,3,2,1,0:T(8,128)S(1)} fusion(f32[1,1,8,8,128]{4,3,2,1,0:T(8,128)S(1)} %get-tuple-element.290, f32[1,1,8,8,128]{4,3,2,1,0:T(8,128)S(1)} %get-tuple-element.289, f32[1,1,8,8,128]{4,3,2,1,0:T(8,128)S(1)} %get-tuple-element.286, f32[1,1,8,8,128]{4,3,2,1,0:T(8,128)S(1)} %get-tuple-element.285, ...), kind=kLoop, calls=%fused_computation.1256 | loop fusion | flops 770048 | bytes 1114176 | tf_op jit(solution)/shard_map/add | solution.py:144
  482.6 35.2 %all_gather.4 = f32[8,2,8,8,128]{4,3,2,1,0:T(8,128)S(1)} all-gather(f32[1,2,8,8,128]{4,3,2,1,0:T(8,128)S(1)} %fusion.647), channel_id=1, replica_groups=mesh['sta'=8,'gx'=4,'gy'=4] {'sta'}, dimensions={0}, use_global_device_ids=true | all-gather | bytes 589824 | tf_op jit(solution)/shard_map/all_gather | solution.py:147
  (409 shorter events, 203.7 us)
Async XLA Ops:
  6.5 339.1 %all-reduce.19.cloned.1.call-start = ((), (), s32[]{:S(2)}) async-start(), calls=%async_computation | async-start | bytes 3145728 | tf_op jit(solution)/shard_map/psum | solution.py:29
  7.7 9.9 %collective-permute-start = (f32[4,6,2,8,128]{4,3,2,0,1:T(8,128)S(1)}, f32[4,6,2,8,128]{4,3,2,0,1:T(8,128)S(1)}, u32[]{:S(2)}, u32[]{:S(2)}) collective-permute-start(f32[4,6,2,8,128]{4,3,2,0,1:T(8,128)S(1)} %copy.83), channel_id=1, source_target_pairs={{0,4},{4,8},{8,12},{1,5},{5,9},{9,13},{2,6},{6,10},{10,14},{3,7},{... | collective-permute-start | bytes 589832 | tf_op jit(solution)/shard_map/ppermute | solution.py:19
  11.6 8.4 %collective-permute-start.1 = (f32[4,6,2,8,128]{4,3,2,0,1:T(8,128)S(1)}, f32[4,6,2,8,128]{4,3,2,0,1:T(8,128)S(1)}, u32[]{:S(2)}, u32[]{:S(2)}) collective-permute-start(f32[4,6,2,8,128]{4,3,2,0,1:T(8,128)S(1)} %copy.85), channel_id=1, source_target_pairs={{4,0},{8,4},{12,8},{5,1},{9,5},{13,9},{6,2},{10,6},{14,10},{7,3},{... | collective-permute-start | bytes 589832 | tf_op jit(solution)/shard_map/ppermute | solution.py:22
  20.2 8.0 %collective-permute-start.2 = (f32[4,6,12,2,128]{4,3,2,0,1:T(2,128)S(1)}, f32[4,6,12,2,128]{4,3,2,0,1:T(2,128)S(1)}, u32[]{:S(2)}, u32[]{:S(2)}) collective-permute-start(f32[4,6,12,2,128]{4,3,2,0,1:T(2,128)S(1)} %get-tuple-element.195), channel_id=1, source_target_pairs={{0,1},{1,2},{2,3},{4,5},{5,6},{6,7},{8,9},{9,10},{10,11},{12,13},{... | collective-permute-start | bytes 884744 | tf_op jit(solution)/shard_map/ppermute | solution.py:19
  22.2 7.9 %collective-permute-start.3 = (f32[4,6,12,2,128]{4,3,2,0,1:T(2,128)S(1)}, f32[4,6,12,2,128]{4,3,2,0,1:T(2,128)S(1)}, u32[]{:S(2)}, u32[]{:S(2)}) collective-permute-start(f32[4,6,12,2,128]{4,3,2,0,1:T(2,128)S(1)} %get-tuple-element.196), channel_id=1, source_target_pairs={{1,0},{2,1},{3,2},{5,4},{6,5},{7,6},{9,8},{10,9},{11,10},{13,12},{... | collective-permute-start | bytes 884744 | tf_op jit(solution)/shard_map/ppermute | solution.py:22
  38.4 6.5 %collective-permute-start.5 = (f32[4,3,2,8,128]{4,3,2,0,1:T(8,128)S(1)}, f32[4,3,2,8,128]{4,3,2,0,1:T(8,128)S(1)}, u32[]{:S(2)}, u32[]{:S(2)}) collective-permute-start(f32[4,3,2,8,128]{4,3,2,0,1:T(8,128)S(1)} %get-tuple-element.292), channel_id=1, source_target_pairs={{4,0},{8,4},{12,8},{5,1},{9,5},{13,9},{6,2},{10,6},{14,10},{7,3},{... | collective-permute-start | bytes 294920 | tf_op jit(solution)/shard_map/ppermute | solution.py:22
  45.0 6.5 %collective-permute-start.6 = (f32[4,3,12,2,128]{4,3,2,0,1:T(2,128)S(1)}, f32[4,3,12,2,128]{4,3,2,0,1:T(2,128)S(1)}, u32[]{:S(2)}, u32[]{:S(2)}) collective-permute-start(f32[4,3,12,2,128]{4,3,2,0,1:T(2,128)S(1)} %get-tuple-element.243), channel_id=1, source_target_pairs={{0,1},{1,2},{2,3},{4,5},{5,6},{6,7},{8,9},{9,10},{10,11},{12,13},{... | collective-permute-start | bytes 442376 | tf_op jit(solution)/shard_map/ppermute | solution.py:19
  47.0 6.3 %collective-permute-start.7 = (f32[4,3,12,2,128]{4,3,2,0,1:T(2,128)S(1)}, f32[4,3,12,2,128]{4,3,2,0,1:T(2,128)S(1)}, u32[]{:S(2)}, u32[]{:S(2)}) collective-permute-start(f32[4,3,12,2,128]{4,3,2,0,1:T(2,128)S(1)} %get-tuple-element.244), channel_id=1, source_target_pairs={{1,0},{2,1},{3,2},{5,4},{6,5},{7,6},{9,8},{10,9},{11,10},{13,12},{... | collective-permute-start | bytes 442376 | tf_op jit(solution)/shard_map/ppermute | solution.py:22
  57.2 6.7 %collective-permute-start.8 = (f32[4,6,2,8,128]{4,3,2,0,1:T(8,128)S(1)}, f32[4,6,2,8,128]{4,3,2,0,1:T(8,128)S(1)}, u32[]{:S(2)}, u32[]{:S(2)}) collective-permute-start(f32[4,6,2,8,128]{4,3,2,0,1:T(8,128)S(1)} %get-tuple-element.211), channel_id=1, source_target_pairs={{0,4},{4,8},{8,12},{1,5},{5,9},{9,13},{2,6},{6,10},{10,14},{3,7},{... | collective-permute-start | bytes 589832 | tf_op jit(solution)/shard_map/ppermute | solution.py:19
  60.8 7.6 %collective-permute-start.9 = (f32[4,6,2,8,128]{4,3,2,0,1:T(8,128)S(1)}, f32[4,6,2,8,128]{4,3,2,0,1:T(8,128)S(1)}, u32[]{:S(2)}, u32[]{:S(2)}) collective-permute-start(f32[4,6,2,8,128]{4,3,2,0,1:T(8,128)S(1)} %get-tuple-element.212), channel_id=1, source_target_pairs={{4,0},{8,4},{12,8},{5,1},{9,5},{13,9},{6,2},{10,6},{14,10},{7,3},{... | collective-permute-start | bytes 589832 | tf_op jit(solution)/shard_map/ppermute | solution.py:22
  68.5 8.0 %collective-permute-start.10 = (f32[4,6,12,2,128]{4,3,2,0,1:T(2,128)S(1)}, f32[4,6,12,2,128]{4,3,2,0,1:T(2,128)S(1)}, u32[]{:S(2)}, u32[]{:S(2)}) collective-permute-start(f32[4,6,12,2,128]{4,3,2,0,1:T(2,128)S(1)} %get-tuple-element.191), channel_id=1, source_target_pairs={{0,1},{1,2},{2,3},{4,5},{5,6},{6,7},{8,9},{9,10},{10,11},{12,13},{... | collective-permute-start | bytes 884744 | tf_op jit(solution)/shard_map/ppermute | solution.py:19
  70.4 7.9 %collective-permute-start.11 = (f32[4,6,12,2,128]{4,3,2,0,1:T(2,128)S(1)}, f32[4,6,12,2,128]{4,3,2,0,1:T(2,128)S(1)}, u32[]{:S(2)}, u32[]{:S(2)}) collective-permute-start(f32[4,6,12,2,128]{4,3,2,0,1:T(2,128)S(1)} %get-tuple-element.192), channel_id=1, source_target_pairs={{1,0},{2,1},{3,2},{5,4},{6,5},{7,6},{9,8},{10,9},{11,10},{13,12},{... | collective-permute-start | bytes 884744 | tf_op jit(solution)/shard_map/ppermute | solution.py:22
  86.7 6.5 %collective-permute-start.13 = (f32[4,3,2,8,128]{4,3,2,0,1:T(8,128)S(1)}, f32[4,3,2,8,128]{4,3,2,0,1:T(8,128)S(1)}, u32[]{:S(2)}, u32[]{:S(2)}) collective-permute-start(f32[4,3,2,8,128]{4,3,2,0,1:T(8,128)S(1)} %get-tuple-element.288), channel_id=1, source_target_pairs={{4,0},{8,4},{12,8},{5,1},{9,5},{13,9},{6,2},{10,6},{14,10},{7,3},{... | collective-permute-start | bytes 294920 | tf_op jit(solution)/shard_map/ppermute | solution.py:22
  93.3 6.5 %collective-permute-start.14 = (f32[4,3,12,2,128]{4,3,2,0,1:T(2,128)S(1)}, f32[4,3,12,2,128]{4,3,2,0,1:T(2,128)S(1)}, u32[]{:S(2)}, u32[]{:S(2)}) collective-permute-start(f32[4,3,12,2,128]{4,3,2,0,1:T(2,128)S(1)} %get-tuple-element.241), channel_id=1, source_target_pairs={{0,1},{1,2},{2,3},{4,5},{5,6},{6,7},{8,9},{9,10},{10,11},{12,13},{... | collective-permute-start | bytes 442376 | tf_op jit(solution)/shard_map/ppermute | solution.py:19
  107.4 7.6 %collective-permute-start.17 = (f32[4,6,2,8,128]{4,3,2,0,1:T(8,128)S(1)}, f32[4,6,2,8,128]{4,3,2,0,1:T(8,128)S(1)}, u32[]{:S(2)}, u32[]{:S(2)}) collective-permute-start(f32[4,6,2,8,128]{4,3,2,0,1:T(8,128)S(1)} %get-tuple-element.210), channel_id=1, source_target_pairs={{4,0},{8,4},{12,8},{5,1},{9,5},{13,9},{6,2},{10,6},{14,10},{7,3},{... | collective-permute-start | bytes 589832 | tf_op jit(solution)/shard_map/ppermute | solution.py:22
  115.2 8.0 %collective-permute-start.18 = (f32[4,6,12,2,128]{4,3,2,0,1:T(2,128)S(1)}, f32[4,6,12,2,128]{4,3,2,0,1:T(2,128)S(1)}, u32[]{:S(2)}, u32[]{:S(2)}) collective-permute-start(f32[4,6,12,2,128]{4,3,2,0,1:T(2,128)S(1)} %get-tuple-element.189), channel_id=1, source_target_pairs={{0,1},{1,2},{2,3},{4,5},{5,6},{6,7},{8,9},{9,10},{10,11},{12,13},{... | collective-permute-start | bytes 884744 | tf_op jit(solution)/shard_map/ppermute | solution.py:19
  117.1 7.9 %collective-permute-start.19 = (f32[4,6,12,2,128]{4,3,2,0,1:T(2,128)S(1)}, f32[4,6,12,2,128]{4,3,2,0,1:T(2,128)S(1)}, u32[]{:S(2)}, u32[]{:S(2)}) collective-permute-start(f32[4,6,12,2,128]{4,3,2,0,1:T(2,128)S(1)} %get-tuple-element.190), channel_id=1, source_target_pairs={{1,0},{2,1},{3,2},{5,4},{6,5},{7,6},{9,8},{10,9},{11,10},{13,12},{... | collective-permute-start | bytes 884744 | tf_op jit(solution)/shard_map/ppermute | solution.py:22
  133.0 6.5 %collective-permute-start.21 = (f32[4,3,2,8,128]{4,3,2,0,1:T(8,128)S(1)}, f32[4,3,2,8,128]{4,3,2,0,1:T(8,128)S(1)}, u32[]{:S(2)}, u32[]{:S(2)}) collective-permute-start(f32[4,3,2,8,128]{4,3,2,0,1:T(8,128)S(1)} %get-tuple-element.284), channel_id=1, source_target_pairs={{4,0},{8,4},{12,8},{5,1},{9,5},{13,9},{6,2},{10,6},{14,10},{7,3},{... | collective-permute-start | bytes 294920 | tf_op jit(solution)/shard_map/ppermute | solution.py:22
  139.6 6.5 %collective-permute-start.22 = (f32[4,3,12,2,128]{4,3,2,0,1:T(2,128)S(1)}, f32[4,3,12,2,128]{4,3,2,0,1:T(2,128)S(1)}, u32[]{:S(2)}, u32[]{:S(2)}) collective-permute-start(f32[4,3,12,2,128]{4,3,2,0,1:T(2,128)S(1)} %get-tuple-element.239), channel_id=1, source_target_pairs={{0,1},{1,2},{2,3},{4,5},{5,6},{6,7},{8,9},{9,10},{10,11},{12,13},{... | collective-permute-start | bytes 442376 | tf_op jit(solution)/shard_map/ppermute | solution.py:19
  153.7 7.6 %collective-permute-start.25 = (f32[4,6,2,8,128]{4,3,2,0,1:T(8,128)S(1)}, f32[4,6,2,8,128]{4,3,2,0,1:T(8,128)S(1)}, u32[]{:S(2)}, u32[]{:S(2)}) collective-permute-start(f32[4,6,2,8,128]{4,3,2,0,1:T(8,128)S(1)} %get-tuple-element.208), channel_id=1, source_target_pairs={{4,0},{8,4},{12,8},{5,1},{9,5},{13,9},{6,2},{10,6},{14,10},{7,3},{... | collective-permute-start | bytes 589832 | tf_op jit(solution)/shard_map/ppermute | solution.py:22
  161.4 8.0 %collective-permute-start.26 = (f32[4,6,12,2,128]{4,3,2,0,1:T(2,128)S(1)}, f32[4,6,12,2,128]{4,3,2,0,1:T(2,128)S(1)}, u32[]{:S(2)}, u32[]{:S(2)}) collective-permute-start(f32[4,6,12,2,128]{4,3,2,0,1:T(2,128)S(1)} %get-tuple-element.187), channel_id=1, source_target_pairs={{0,1},{1,2},{2,3},{4,5},{5,6},{6,7},{8,9},{9,10},{10,11},{12,13},{... | collective-permute-start | bytes 884744 | tf_op jit(solution)/shard_map/ppermute | solution.py:19
  163.4 7.9 %collective-permute-start.27 = (f32[4,6,12,2,128]{4,3,2,0,1:T(2,128)S(1)}, f32[4,6,12,2,128]{4,3,2,0,1:T(2,128)S(1)}, u32[]{:S(2)}, u32[]{:S(2)}) collective-permute-start(f32[4,6,12,2,128]{4,3,2,0,1:T(2,128)S(1)} %get-tuple-element.188), channel_id=1, source_target_pairs={{1,0},{2,1},{3,2},{5,4},{6,5},{7,6},{9,8},{10,9},{11,10},{13,12},{... | collective-permute-start | bytes 884744 | tf_op jit(solution)/shard_map/ppermute | solution.py:22
  179.3 6.5 %collective-permute-start.29 = (f32[4,3,2,8,128]{4,3,2,0,1:T(8,128)S(1)}, f32[4,3,2,8,128]{4,3,2,0,1:T(8,128)S(1)}, u32[]{:S(2)}, u32[]{:S(2)}) collective-permute-start(f32[4,3,2,8,128]{4,3,2,0,1:T(8,128)S(1)} %get-tuple-element.280), channel_id=1, source_target_pairs={{4,0},{8,4},{12,8},{5,1},{9,5},{13,9},{6,2},{10,6},{14,10},{7,3},{... | collective-permute-start | bytes 294920 | tf_op jit(solution)/shard_map/ppermute | solution.py:22
  185.9 6.5 %collective-permute-start.30 = (f32[4,3,12,2,128]{4,3,2,0,1:T(2,128)S(1)}, f32[4,3,12,2,128]{4,3,2,0,1:T(2,128)S(1)}, u32[]{:S(2)}, u32[]{:S(2)}) collective-permute-start(f32[4,3,12,2,128]{4,3,2,0,1:T(2,128)S(1)} %get-tuple-element.237), channel_id=1, source_target_pairs={{0,1},{1,2},{2,3},{4,5},{5,6},{6,7},{8,9},{9,10},{10,11},{12,13},{... | collective-permute-start | bytes 442376 | tf_op jit(solution)/shard_map/ppermute | solution.py:19
  200.0 7.6 %collective-permute-start.33 = (f32[4,6,2,8,128]{4,3,2,0,1:T(8,128)S(1)}, f32[4,6,2,8,128]{4,3,2,0,1:T(8,128)S(1)}, u32[]{:S(2)}, u32[]{:S(2)}) collective-permute-start(f32[4,6,2,8,128]{4,3,2,0,1:T(8,128)S(1)} %get-tuple-element.206), channel_id=1, source_target_pairs={{4,0},{8,4},{12,8},{5,1},{9,5},{13,9},{6,2},{10,6},{14,10},{7,3},{... | collective-permute-start | bytes 589832 | tf_op jit(solution)/shard_map/ppermute | solution.py:22
  208.6 13.5 %collective-permute-start.34 = (f32[4,6,12,2,128]{4,3,2,0,1:T(2,128)}, f32[4,6,12,2,128]{4,3,2,0,1:T(2,128)S(1)}, u32[]{:S(2)}, u32[]{:S(2)}) collective-permute-start(f32[4,6,12,2,128]{4,3,2,0,1:T(2,128)} %get-tuple-element.185), channel_id=1, source_target_pairs={{0,1},{1,2},{2,3},{4,5},{5,6},{6,7},{8,9},{9,10},{10,11},{12,13},{... | collective-permute-start | bytes 884744 | tf_op jit(solution)/shard_map/ppermute | solution.py:19
  210.5 11.6 %collective-permute-start.35 = (f32[4,6,12,2,128]{4,3,2,0,1:T(2,128)}, f32[4,6,12,2,128]{4,3,2,0,1:T(2,128)}, u32[]{:S(2)}, u32[]{:S(2)}) collective-permute-start(f32[4,6,12,2,128]{4,3,2,0,1:T(2,128)} %get-tuple-element.186), channel_id=1, source_target_pairs={{1,0},{2,1},{3,2},{5,4},{6,5},{7,6},{9,8},{10,9},{11,10},{13,12},{... | collective-permute-start | bytes 884744 | tf_op jit(solution)/shard_map/ppermute | solution.py:22
  230.7 8.6 %collective-permute-start.36 = (f32[4,3,2,8,128]{4,3,2,0,1:T(8,128)}, f32[4,3,2,8,128]{4,3,2,0,1:T(8,128)S(1)}, u32[]{:S(2)}, u32[]{:S(2)}) collective-permute-start(f32[4,3,2,8,128]{4,3,2,0,1:T(8,128)} %get-tuple-element.275), channel_id=1, source_target_pairs={{0,4},{4,8},{8,12},{1,5},{5,9},{9,13},{2,6},{6,10},{10,14},{3,7},{... | collective-permute-start | bytes 294920 | tf_op jit(solution)/shard_map/ppermute | solution.py:19
  232.7 6.7 %collective-permute-start.37 = (f32[4,3,2,8,128]{4,3,2,0,1:T(8,128)S(1)}, f32[4,3,2,8,128]{4,3,2,0,1:T(8,128)S(1)}, u32[]{:S(2)}, u32[]{:S(2)}) collective-permute-start(f32[4,3,2,8,128]{4,3,2,0,1:T(8,128)S(1)} %get-tuple-element.276), channel_id=1, source_target_pairs={{4,0},{8,4},{12,8},{5,1},{9,5},{13,9},{6,2},{10,6},{14,10},{7,3},{... | collective-permute-start | bytes 294920 | tf_op jit(solution)/shard_map/ppermute | solution.py:22
  240.2 7.7 %collective-permute-start.38 = (f32[4,3,12,2,128]{4,3,2,0,1:T(2,128)}, f32[4,3,12,2,128]{4,3,2,0,1:T(2,128)}, u32[]{:S(2)}, u32[]{:S(2)}) collective-permute-start(f32[4,3,12,2,128]{4,3,2,0,1:T(2,128)} %get-tuple-element.235), channel_id=1, source_target_pairs={{0,1},{1,2},{2,3},{4,5},{5,6},{6,7},{8,9},{9,10},{10,11},{12,13},{... | collective-permute-start | bytes 442376 | tf_op jit(solution)/shard_map/ppermute | solution.py:19
  242.1 6.6 %collective-permute-start.39 = (f32[4,3,12,2,128]{4,3,2,0,1:T(2,128)}, f32[4,3,12,2,128]{4,3,2,0,1:T(2,128)}, u32[]{:S(2)}, u32[]{:S(2)}) collective-permute-start(f32[4,3,12,2,128]{4,3,2,0,1:T(2,128)} %get-tuple-element.236), channel_id=1, source_target_pairs={{1,0},{2,1},{3,2},{5,4},{6,5},{7,6},{9,8},{10,9},{11,10},{13,12},{... | collective-permute-start | bytes 442376 | tf_op jit(solution)/shard_map/ppermute | solution.py:22
  254.3 8.0 %collective-permute-start.40 = (f32[4,6,2,8,128]{4,3,2,0,1:T(8,128)}, f32[4,6,2,8,128]{4,3,2,0,1:T(8,128)S(1)}, u32[]{:S(2)}, u32[]{:S(2)}) collective-permute-start(f32[4,6,2,8,128]{4,3,2,0,1:T(8,128)} %get-tuple-element.203), channel_id=1, source_target_pairs={{0,4},{4,8},{8,12},{1,5},{5,9},{9,13},{2,6},{6,10},{10,14},{3,7},{... | collective-permute-start | bytes 589832 | tf_op jit(solution)/shard_map/ppermute | solution.py:19
  258.9 7.6 %collective-permute-start.41 = (f32[4,6,2,8,128]{4,3,2,0,1:T(8,128)S(1)}, f32[4,6,2,8,128]{4,3,2,0,1:T(8,128)S(1)}, u32[]{:S(2)}, u32[]{:S(2)}) collective-permute-start(f32[4,6,2,8,128]{4,3,2,0,1:T(8,128)S(1)} %get-tuple-element.204), channel_id=1, source_target_pairs={{4,0},{8,4},{12,8},{5,1},{9,5},{13,9},{6,2},{10,6},{14,10},{7,3},{... | collective-permute-start | bytes 589832 | tf_op jit(solution)/shard_map/ppermute | solution.py:22
  267.4 80.0 %collective-permute-start.42 = (f32[4,6,12,2,128]{4,3,2,0,1:T(2,128)}, f32[4,6,12,2,128]{4,3,2,0,1:T(2,128)}, u32[]{:S(2)}, u32[]{:S(2)}) collective-permute-start(f32[4,6,12,2,128]{4,3,2,0,1:T(2,128)} %get-tuple-element.183), channel_id=1, source_target_pairs={{0,1},{1,2},{2,3},{4,5},{5,6},{6,7},{8,9},{9,10},{10,11},{12,13},{... | collective-permute-start | bytes 884744 | tf_op jit(solution)/shard_map/ppermute | solution.py:19
  269.4 78.1 %collective-permute-start.43 = (f32[4,6,12,2,128]{4,3,2,0,1:T(2,128)}, f32[4,6,12,2,128]{4,3,2,0,1:T(2,128)}, u32[]{:S(2)}, u32[]{:S(2)}) collective-permute-start(f32[4,6,12,2,128]{4,3,2,0,1:T(2,128)} %get-tuple-element.184), channel_id=1, source_target_pairs={{1,0},{2,1},{3,2},{5,4},{6,5},{7,6},{9,8},{10,9},{11,10},{13,12},{... | collective-permute-start | bytes 884744 | tf_op jit(solution)/shard_map/ppermute | solution.py:22
  359.2 6.5 %collective-permute-start.45 = (f32[4,3,2,8,128]{4,3,2,0,1:T(8,128)S(1)}, f32[4,3,2,8,128]{4,3,2,0,1:T(8,128)S(1)}, u32[]{:S(2)}, u32[]{:S(2)}) collective-permute-start(f32[4,3,2,8,128]{4,3,2,0,1:T(8,128)S(1)} %get-tuple-element.272), channel_id=1, source_target_pairs={{4,0},{8,4},{12,8},{5,1},{9,5},{13,9},{6,2},{10,6},{14,10},{7,3},{... | collective-permute-start | bytes 294920 | tf_op jit(solution)/shard_map/ppermute | solution.py:22
  365.8 6.5 %collective-permute-start.46 = (f32[4,3,12,2,128]{4,3,2,0,1:T(2,128)S(1)}, f32[4,3,12,2,128]{4,3,2,0,1:T(2,128)S(1)}, u32[]{:S(2)}, u32[]{:S(2)}) collective-permute-start(f32[4,3,12,2,128]{4,3,2,0,1:T(2,128)S(1)} %get-tuple-element.233), channel_id=1, source_target_pairs={{0,1},{1,2},{2,3},{4,5},{5,6},{6,7},{8,9},{9,10},{10,11},{12,13},{... | collective-permute-start | bytes 442376 | tf_op jit(solution)/shard_map/ppermute | solution.py:19
  377.3 6.8 %collective-permute-start.48 = (f32[4,6,2,8,128]{4,3,2,0,1:T(8,128)S(1)}, f32[4,6,2,8,128]{4,3,2,0,1:T(8,128)S(1)}, u32[]{:S(2)}, u32[]{:S(2)}) collective-permute-start(f32[4,6,2,8,128]{4,3,2,0,1:T(8,128)S(1)} %get-tuple-element.201), channel_id=1, source_target_pairs={{0,4},{4,8},{8,12},{1,5},{5,9},{9,13},{2,6},{6,10},{10,14},{3,7},{... | collective-permute-start | bytes 589832 | tf_op jit(solution)/shard_map/ppermute | solution.py:19
  380.9 7.6 %collective-permute-start.49 = (f32[4,6,2,8,128]{4,3,2,0,1:T(8,128)S(1)}, f32[4,6,2,8,128]{4,3,2,0,1:T(8,128)S(1)}, u32[]{:S(2)}, u32[]{:S(2)}) collective-permute-start(f32[4,6,2,8,128]{4,3,2,0,1:T(8,128)S(1)} %get-tuple-element.202), channel_id=1, source_target_pairs={{4,0},{8,4},{12,8},{5,1},{9,5},{13,9},{6,2},{10,6},{14,10},{7,3},{... | collective-permute-start | bytes 589832 | tf_op jit(solution)/shard_map/ppermute | solution.py:22
  388.6 8.0 %collective-permute-start.50 = (f32[4,6,12,2,128]{4,3,2,0,1:T(2,128)S(1)}, f32[4,6,12,2,128]{4,3,2,0,1:T(2,128)S(1)}, u32[]{:S(2)}, u32[]{:S(2)}) collective-permute-start(f32[4,6,12,2,128]{4,3,2,0,1:T(2,128)S(1)} %get-tuple-element.181), channel_id=1, source_target_pairs={{0,1},{1,2},{2,3},{4,5},{5,6},{6,7},{8,9},{9,10},{10,11},{12,13},{... | collective-permute-start | bytes 884744 | tf_op jit(solution)/shard_map/ppermute | solution.py:19
  390.6 7.9 %collective-permute-start.51 = (f32[4,6,12,2,128]{4,3,2,0,1:T(2,128)S(1)}, f32[4,6,12,2,128]{4,3,2,0,1:T(2,128)S(1)}, u32[]{:S(2)}, u32[]{:S(2)}) collective-permute-start(f32[4,6,12,2,128]{4,3,2,0,1:T(2,128)S(1)} %get-tuple-element.182), channel_id=1, source_target_pairs={{1,0},{2,1},{3,2},{5,4},{6,5},{7,6},{9,8},{10,9},{11,10},{13,12},{... | collective-permute-start | bytes 884744 | tf_op jit(solution)/shard_map/ppermute | solution.py:22
  408.4 6.5 %collective-permute-start.53 = (f32[4,3,2,8,128]{4,3,2,0,1:T(8,128)S(1)}, f32[4,3,2,8,128]{4,3,2,0,1:T(8,128)S(1)}, u32[]{:S(2)}, u32[]{:S(2)}) collective-permute-start(f32[4,3,2,8,128]{4,3,2,0,1:T(8,128)S(1)} %get-tuple-element.268), channel_id=1, source_target_pairs={{4,0},{8,4},{12,8},{5,1},{9,5},{13,9},{6,2},{10,6},{14,10},{7,3},{... | collective-permute-start | bytes 294920 | tf_op jit(solution)/shard_map/ppermute | solution.py:22
  415.0 6.5 %collective-permute-start.54 = (f32[4,3,12,2,128]{4,3,2,0,1:T(2,128)S(1)}, f32[4,3,12,2,128]{4,3,2,0,1:T(2,128)S(1)}, u32[]{:S(2)}, u32[]{:S(2)}) collective-permute-start(f32[4,3,12,2,128]{4,3,2,0,1:T(2,128)S(1)} %get-tuple-element.231), channel_id=1, source_target_pairs={{0,1},{1,2},{2,3},{4,5},{5,6},{6,7},{8,9},{9,10},{10,11},{12,13},{... | collective-permute-start | bytes 442376 | tf_op jit(solution)/shard_map/ppermute | solution.py:19
  428.4 7.6 %collective-permute-start.57 = (f32[4,6,2,8,128]{4,3,2,1,0:T(8,128)S(1)}, f32[4,6,2,8,128]{4,3,2,1,0:T(8,128)S(1)}, u32[]{:S(2)}, u32[]{:S(2)}) collective-permute-start(f32[4,6,2,8,128]{4,3,2,1,0:T(8,128)S(1)} %get-tuple-element.200), channel_id=1, source_target_pairs={{4,0},{8,4},{12,8},{5,1},{9,5},{13,9},{6,2},{10,6},{14,10},{7,3},{... | collective-permute-start | bytes 589832 | tf_op jit(solution)/shard_map/ppermute | solution.py:22
  436.1 8.0 %collective-permute-start.58 = (f32[4,6,12,2,128]{4,3,2,1,0:T(2,128)S(1)}, f32[4,6,12,2,128]{4,3,2,1,0:T(2,128)S(1)}, u32[]{:S(2)}, u32[]{:S(2)}) collective-permute-start(f32[4,6,12,2,128]{4,3,2,1,0:T(2,128)S(1)} %get-tuple-element.179), channel_id=1, source_target_pairs={{0,1},{1,2},{2,3},{4,5},{5,6},{6,7},{8,9},{9,10},{10,11},{12,13},{... | collective-permute-start | bytes 884744 | tf_op jit(solution)/shard_map/ppermute | solution.py:19
  438.1 7.9 %collective-permute-start.59 = (f32[4,6,12,2,128]{4,3,2,1,0:T(2,128)S(1)}, f32[4,6,12,2,128]{4,3,2,1,0:T(2,128)S(1)}, u32[]{:S(2)}, u32[]{:S(2)}) collective-permute-start(f32[4,6,12,2,128]{4,3,2,1,0:T(2,128)S(1)} %get-tuple-element.180), channel_id=1, source_target_pairs={{1,0},{2,1},{3,2},{5,4},{6,5},{7,6},{9,8},{10,9},{11,10},{13,12},{... | collective-permute-start | bytes 884744 | tf_op jit(solution)/shard_map/ppermute | solution.py:22
  454.2 6.5 %collective-permute-start.61 = (f32[4,3,2,8,128]{4,3,2,0,1:T(8,128)S(1)}, f32[4,3,2,8,128]{4,3,2,0,1:T(8,128)S(1)}, u32[]{:S(2)}, u32[]{:S(2)}) collective-permute-start(f32[4,3,2,8,128]{4,3,2,0,1:T(8,128)S(1)} %get-tuple-element.264), channel_id=1, source_target_pairs={{4,0},{8,4},{12,8},{5,1},{9,5},{13,9},{6,2},{10,6},{14,10},{7,3},{... | collective-permute-start | bytes 294920 | tf_op jit(solution)/shard_map/ppermute | solution.py:22
  460.8 6.5 %collective-permute-start.62 = (f32[4,3,12,2,128]{4,3,2,0,1:T(2,128)S(1)}, f32[4,3,12,2,128]{4,3,2,0,1:T(2,128)S(1)}, u32[]{:S(2)}, u32[]{:S(2)}) collective-permute-start(f32[4,3,12,2,128]{4,3,2,0,1:T(2,128)S(1)} %get-tuple-element.229), channel_id=1, source_target_pairs={{0,1},{1,2},{2,3},{4,5},{5,6},{6,7},{8,9},{9,10},{10,11},{12,13},{... | collective-permute-start | bytes 442376 | tf_op jit(solution)/shard_map/ppermute | solution.py:19
  (67 other events, 626.2 us)
Sparse Core Ops, SparseCore 0:
  248.0 97.6 all-reduce.18
